TPU v7x, 32 devices: a whole 2x2x4 slice. The times are simulated.
32 devices in a mesh: dp: 8 (over z, y), tensor: 4 (over x, core).
Axes of the slice: x: 2, y: 2, z: 4, core: 2. Of those that a mesh axis runs over, the one named last changes fastest.
Arguments:
- tokens: bfloat16 [4096, 2048], P(('dp', 'tensor')), may hold values from -6 to 6
- cotangent: bfloat16 [4096, 2048], P(('dp', 'tensor')), may hold values from -6 to 6
- valid_mask: int32 [4096], P(('dp', 'tensor')), may hold values 0 or 1
- seq_lengths: int32 [4], replicated, may hold values from 1 to 2048, 4096 in all
- block_order: int32 [32], replicated, may hold values from 0 to 31, each once
- norm_gain1: float32 [2048], P(('dp', 'tensor')), may hold values from 0.5 to 1.5
- w_input: bfloat16 [2048, 2048], P('dp', 'tensor'), may hold values from -0.125 to 0.125
- w_forget: bfloat16 [2048, 2048], P('dp', 'tensor'), may hold values from -0.125 to 0.125
- w_gate_mix: bfloat16 [2048, 2048], P('dp', 'tensor'), may hold values from -0.125 to 0.125
- forget_bias: float32 [2048], P(('dp', 'tensor')), may hold values from -2 to 8
- out_gain: float32 [2048], P(('dp', 'tensor')), may hold values from 0.5 to 1.5
- w_out: bfloat16 [2048, 2048], P('tensor', 'dp'), may hold values from -0.1875 to 0.1875
- norm_gain2: float32 [2048], P(('dp', 'tensor')), may hold values from 0.5 to 1.5
- w_gate: bfloat16 [2048, 5632], P('dp', 'tensor'), may hold values from -0.125 to 0.125
- w_up: bfloat16 [2048, 5632], P('dp', 'tensor'), may hold values from -0.125 to 0.125
- w_down: bfloat16 [5632, 2048], P('tensor', 'dp'), may hold values from -0.15625 to 0.15625
Outputs:
- layer_out: bfloat16 [4096, 2048], P(('dp', 'tensor'))
- input_grad: bfloat16 [4096, 2048], P(('dp', 'tensor'))
- grad_norm_gain1: float32 [2048], P(('dp', 'tensor'))
- grad_w_input: float32 [2048, 2048], P('dp', 'tensor')
- grad_w_forget: float32 [2048, 2048], P('dp', 'tensor')
- grad_w_gate_mix: float32 [2048, 2048], P('dp', 'tensor')
- grad_forget_bias: float32 [2048], P(('dp', 'tensor'))
- grad_out_gain: float32 [2048], P(('dp', 'tensor'))
- grad_w_out: float32 [2048, 2048], P('tensor', 'dp')
- grad_norm_gain2: float32 [2048], P(('dp', 'tensor'))
- grad_w_gate: float32 [2048, 5632], P('dp', 'tensor')
- grad_w_up: float32 [2048, 5632], P('dp', 'tensor')
- grad_w_down: float32 [5632, 2048], P('tensor', 'dp')
- rms_stats: float32 [3], replicated
Inputs may be any that keep to these rules, and one draw needn't show every extreme that they name: `seq_lengths`: 4 packed sequences in pack order that cover all 4096 tokens; the longest has exactly 2048 tokens. `block_order`: entry j names the block of 128 pack tokens held by dealt block j; every block once.
All inputs are finite; a program needn't handle non-finite values. No bound on the sum of `valid_mask` on one device may be relied on, other than what follows from the above.
Results may differ from a plain program's by a relative error of at most 0.0095.
Values may be sent and summed in bfloat16 or wider, within the bound.
A program may use at most 192 MiB of HBM per device.

v0:
```python
import jax
import jax.numpy as jnp
from jax import lax
from jax.sharding import PartitionSpec as P

D = 2048
BLOCK = 128


epsilon = 1e-06
lower_bound = 0.75


def linear_step(earlier, current):
    return (earlier[0] * current[0], current[0] * earlier[1] + current[1])


def row_scale(values):
    return lax.rsqrt(jnp.mean(values * values, axis=1, keepdims=True) + epsilon)


def times_transposed(operand, matrix):
    return lax.dot_general(
        operand, matrix, (((1,), (1,)), ((), ())), preferred_element_type=jnp.float32
    )


def inner_rows(operand, matrix):
    return lax.dot_general(
        operand, matrix, (((0,), (0,)), ((), ())), preferred_element_type=jnp.float32
    )


def silu_slope(values, sigmoid_value):
    return sigmoid_value * (1.0 + values * (1.0 - sigmoid_value))


def norm_back(grad_normed, scaled_rows, row_factor, gain_vector):
    grad_scaled = grad_normed * gain_vector
    mean_term = jnp.mean(grad_scaled * scaled_rows, axis=1, keepdims=True)
    return (
        row_factor * (grad_scaled - scaled_rows * mean_term),
        jnp.sum(grad_normed * scaled_rows, axis=0),
    )


def ordered(values, block_order):
    return jnp.zeros_like(values).at[block_order].set(values)


def entering_state(decays, states, block_order):
    total_decay, total_state = lax.associative_scan(
        linear_step, (ordered(decays, block_order), ordered(states, block_order)), axis=0
    )
    return jnp.concatenate([jnp.zeros_like(total_state[:1]), total_state[:-1]], axis=0)


def entering_grad(decays, grads_in, block_order):
    total_decay, total_grad = lax.associative_scan(
        linear_step,
        (ordered(decays, block_order), ordered(grads_in, block_order)),
        axis=0,
        reverse=True,
    )
    return jnp.concatenate([total_grad[1:], jnp.zeros_like(total_grad[:1])], axis=0)


def widen(values, channel_start):
    return lax.dynamic_update_slice_in_dim(jnp.zeros((D,), jnp.float32), values, channel_start, 0)


def tensor_rows(values):
    return lax.all_gather(values, "tensor", axis=0, tiled=True)


def tensor_reduce(partial_term, row_count):
    return lax.psum_scatter(
        partial_term(jnp.int32(0), row_count * lax.axis_size("tensor")),
        "tensor",
        scatter_dimension=0,
        tiled=True,
    )


def row_total(values):
    return lax.psum(values, "tensor")


def shards(
    tokens,
    cotangent,
    valid_mask,
    seq_lengths,
    block_order,
    norm_gain1,
    w_input,
    w_forget,
    w_gate_mix,
    forget_bias,
    out_gain,
    w_out,
    norm_gain2,
    w_gate,
    w_up,
    w_down,
):
    tensor_count = lax.axis_size("tensor")
    dp_index = lax.axis_index("dp")
    tensor_index = lax.axis_index("tensor")
    own_rows = tokens.shape[0]
    group_rows = own_rows * tensor_count
    blocks_here = group_rows // BLOCK
    width_local = w_input.shape[1]
    channel_start = tensor_index * width_local
    small_full = (
        lax.all_gather(norm_gain1, ("dp", "tensor"), axis=0, tiled=True),
        lax.all_gather(forget_bias, ("dp", "tensor"), axis=0, tiled=True),
        lax.all_gather(out_gain, ("dp", "tensor"), axis=0, tiled=True),
        lax.all_gather(norm_gain2, ("dp", "tensor"), axis=0, tiled=True),
    )
    gain_first = small_full[0]
    bias_local = lax.dynamic_slice_in_dim(small_full[1], channel_start, width_local)
    gain_out = lax.dynamic_slice_in_dim(small_full[2], channel_start, width_local)
    gain_second = small_full[3]
    full_weights = (
        lax.all_gather(w_input, "dp", axis=0, tiled=True),
        lax.all_gather(w_forget, "dp", axis=0, tiled=True),
        lax.all_gather(w_gate_mix, "dp", axis=0, tiled=True),
        lax.all_gather(w_out, "dp", axis=1, tiled=True),
        lax.all_gather(w_gate, "dp", axis=0, tiled=True),
        lax.all_gather(w_up, "dp", axis=0, tiled=True),
        lax.all_gather(w_down, "dp", axis=1, tiled=True),
    )
    weight_input, weight_forget, weight_mix, weight_out, weight_gate, weight_up, weight_down = (
        full_weights
    )
    block_ids = lax.dynamic_slice_in_dim(block_order, dp_index * blocks_here, blocks_here)
    positions = block_ids[:, None] * BLOCK + jnp.arange(BLOCK, dtype=jnp.int32)[None, :]
    seq_starts = jnp.cumsum(seq_lengths) - seq_lengths
    is_start = jnp.any(positions[:, :, None] == seq_starts[None, None, :], axis=2)
    keep_flag = jnp.where(is_start, 0.0, 1.0).astype(jnp.float32).reshape(group_rows, 1)
    stream = tokens.astype(jnp.float32)
    scale_first = row_scale(stream)
    scaled_first = stream * scale_first
    mixer_in = tensor_rows((scaled_first * gain_first).astype(jnp.bfloat16))
    input_raw = jnp.dot(mixer_in, weight_input, preferred_element_type=jnp.float32)
    forget_raw = jnp.dot(mixer_in, weight_forget, preferred_element_type=jnp.float32)
    gate_raw = jnp.dot(mixer_in, weight_mix, preferred_element_type=jnp.float32)
    forget_sigma = jax.nn.sigmoid(forget_raw + bias_local)
    forget_gate = lower_bound + (1.0 - lower_bound) * forget_sigma
    input_sigma = jax.nn.sigmoid(input_raw)
    input_act = input_raw * input_sigma
    increment = input_act * (1.0 - forget_gate)
    decay_rate = forget_gate * keep_flag
    decay_blocks = decay_rate.reshape(blocks_here, BLOCK, width_local)
    cum_decay, local_state = lax.associative_scan(
        linear_step, (decay_blocks, increment.reshape(blocks_here, BLOCK, width_local)), axis=1
    )
    block_decay, block_state = (
        lax.all_gather(cum_decay[:, -1], "dp", axis=0, tiled=True),
        lax.all_gather(local_state[:, -1], "dp", axis=0, tiled=True),
    )
    carry_in = entering_state(block_decay, block_state, block_order)[block_ids]
    hidden_blocks = local_state + cum_decay * carry_in[:, None, :]
    prev_state = jnp.concatenate([carry_in[:, None, :], hidden_blocks[:, :-1]], axis=1).reshape(
        group_rows, width_local
    )
    hidden_state = hidden_blocks.reshape(group_rows, width_local)
    square_total = row_total(jnp.sum(hidden_state * hidden_state, axis=1))
    state_scale = lax.rsqrt(square_total / D + epsilon)[:, None]
    state_normed = hidden_state * state_scale
    gate_sigma = jax.nn.sigmoid(gate_raw)
    gate_act = gate_raw * gate_sigma
    mixer_cast = (state_normed * gain_out * gate_act).astype(jnp.bfloat16)

    def mixer_term(row_start, row_count):
        return jnp.dot(mixer_cast, weight_out, preferred_element_type=jnp.float32)

    mixer_out = tensor_reduce(mixer_term, own_rows)
    after_mixer = stream + mixer_out
    scale_second = row_scale(after_mixer)
    scaled_second = after_mixer * scale_second
    ffn_in = tensor_rows((scaled_second * gain_second).astype(jnp.bfloat16))
    gate_pre = jnp.dot(ffn_in, weight_gate, preferred_element_type=jnp.float32)
    up_pre = jnp.dot(ffn_in, weight_up, preferred_element_type=jnp.float32)
    gate_sig = jax.nn.sigmoid(gate_pre)
    hidden_units = (gate_pre * gate_sig * up_pre).astype(jnp.bfloat16)

    def ffn_term(row_start, row_count):
        return jnp.dot(hidden_units, weight_down, preferred_element_type=jnp.float32)

    ffn_out = tensor_reduce(ffn_term, own_rows)
    residual_sum = after_mixer + ffn_out
    valid_rows = valid_mask.astype(jnp.float32)
    totals = lax.psum(
        (
            jnp.sum(valid_rows * jnp.sum(residual_sum * residual_sum, axis=1)),
            jnp.sum(valid_rows * jnp.sum(mixer_out * mixer_out, axis=1)),
            jnp.sum(valid_rows * jnp.sum(ffn_out * ffn_out, axis=1)),
            jnp.sum(valid_rows),
        ),
        ("dp", "tensor"),
    )
    divisor = jnp.maximum(totals[3], 1.0) * D
    rms_stats = jnp.sqrt(jnp.stack([totals[0], totals[1], totals[2]]) / divisor)
    back_weights = (
        lax.all_gather(w_input, "dp", axis=0, tiled=True),
        lax.all_gather(w_forget, "dp", axis=0, tiled=True),
        lax.all_gather(w_gate_mix, "dp", axis=0, tiled=True),
        lax.all_gather(w_out, "dp", axis=1, tiled=True),
        lax.all_gather(w_gate, "dp", axis=0, tiled=True),
        lax.all_gather(w_up, "dp", axis=0, tiled=True),
        lax.all_gather(w_down, "dp", axis=1, tiled=True),
    )
    input_back, forget_back, mix_back, out_back, gate_back, up_back, down_back = back_weights
    grad_out = cotangent.astype(jnp.float32) * valid_rows[:, None]
    grad_ffn_all = tensor_rows(grad_out.astype(jnp.bfloat16))
    grad_hidden = times_transposed(grad_ffn_all, down_back)
    grad_gate_pre = (grad_hidden * up_pre * silu_slope(gate_pre, gate_sig)).astype(jnp.bfloat16)
    grad_up_pre = (grad_hidden * gate_pre * gate_sig).astype(jnp.bfloat16)
    grad_down = inner_rows(hidden_units, grad_ffn_all)
    grad_gate = inner_rows(ffn_in, grad_gate_pre)
    grad_up = inner_rows(ffn_in, grad_up_pre)

    def ffn_back_term(row_start, row_count):
        return times_transposed(grad_gate_pre, gate_back) + times_transposed(grad_up_pre, up_back)

    grad_normed_second = tensor_reduce(ffn_back_term, own_rows)
    grad_stream_second, grad_gain_second = norm_back(
        grad_normed_second, scaled_second, scale_second, gain_second
    )
    grad_after = grad_out + grad_stream_second
    grad_mix_all = tensor_rows(grad_after.astype(jnp.bfloat16))
    grad_mixed = times_transposed(grad_mix_all, out_back)
    grad_wout = inner_rows(mixer_cast, grad_mix_all)
    grad_gain_out_local = jnp.sum(grad_mixed * state_normed * gate_act, axis=0)
    grad_gate_raw = (
        grad_mixed * state_normed * gain_out * silu_slope(gate_raw, gate_sigma)
    ).astype(jnp.bfloat16)
    grad_normed_state = grad_mixed * gain_out * gate_act
    cross_total = row_total(jnp.sum(grad_normed_state * state_normed, axis=1))
    grad_direct = state_scale * (grad_normed_state - state_normed * (cross_total / D)[:, None])
    decay_next = jnp.concatenate([decay_blocks[:, 1:], jnp.ones_like(decay_blocks[:, :1])], axis=1)
    tail_decay, tail_grad = lax.associative_scan(
        linear_step,
        (decay_next, grad_direct.reshape(blocks_here, BLOCK, width_local)),
        axis=1,
        reverse=True,
    )
    head_decay = decay_blocks[:, 0]
    pass_decay, pass_grad = (
        lax.all_gather(head_decay * tail_decay[:, 0], "dp", axis=0, tiled=True),
        lax.all_gather(head_decay * tail_grad[:, 0], "dp", axis=0, tiled=True),
    )
    carry_back = entering_grad(pass_decay, pass_grad, block_order)[block_ids]
    state_grad = (tail_grad + tail_decay * carry_back[:, None, :]).reshape(group_rows, width_local)
    grad_forget_gate = keep_flag * state_grad * prev_state - state_grad * input_act
    grad_forget_pre = grad_forget_gate * (1.0 - lower_bound) * forget_sigma * (1.0 - forget_sigma)
    grad_bias_local = jnp.sum(grad_forget_pre, axis=0)
    grad_input_raw = (state_grad * (1.0 - forget_gate) * silu_slope(input_raw, input_sigma)).astype(
        jnp.bfloat16
    )
    grad_forget_raw = grad_forget_pre.astype(jnp.bfloat16)
    grad_winput = inner_rows(mixer_in, grad_input_raw)
    grad_wforget = inner_rows(mixer_in, grad_forget_raw)
    grad_wmix = inner_rows(mixer_in, grad_gate_raw)

    def mixer_back_term(row_start, row_count):
        total_term = times_transposed(grad_input_raw, input_back)
        total_term = total_term + times_transposed(grad_forget_raw, forget_back)
        return total_term + times_transposed(grad_gate_raw, mix_back)

    grad_normed_first = tensor_reduce(mixer_back_term, own_rows)
    grad_stream_first, grad_gain_first = norm_back(
        grad_normed_first, scaled_first, scale_first, gain_first
    )
    input_grad = (grad_after + grad_stream_first).astype(jnp.bfloat16)
    summed = (
        lax.psum_scatter(grad_winput, "dp", scatter_dimension=0, tiled=True),
        lax.psum_scatter(grad_wforget, "dp", scatter_dimension=0, tiled=True),
        lax.psum_scatter(grad_wmix, "dp", scatter_dimension=0, tiled=True),
        lax.psum_scatter(grad_wout, "dp", scatter_dimension=1, tiled=True),
        lax.psum_scatter(grad_gate, "dp", scatter_dimension=0, tiled=True),
        lax.psum_scatter(grad_up, "dp", scatter_dimension=0, tiled=True),
        lax.psum_scatter(grad_down, "dp", scatter_dimension=1, tiled=True),
    )
    small_summed = (
        lax.psum_scatter(grad_gain_first, ("dp", "tensor"), scatter_dimension=0, tiled=True),
        lax.psum_scatter(
            widen(grad_bias_local, channel_start), ("dp", "tensor"), scatter_dimension=0, tiled=True
        ),
        lax.psum_scatter(
            widen(grad_gain_out_local, channel_start),
            ("dp", "tensor"),
            scatter_dimension=0,
            tiled=True,
        ),
        lax.psum_scatter(grad_gain_second, ("dp", "tensor"), scatter_dimension=0, tiled=True),
    )
    return (
        residual_sum.astype(jnp.bfloat16),
        input_grad,
        small_summed[0],
        summed[0],
        summed[1],
        summed[2],
        small_summed[1],
        small_summed[2],
        summed[3],
        small_summed[3],
        summed[4],
        summed[5],
        summed[6],
        rms_stats,
    )


def solution(mesh):
    placed = (
        P(("dp", "tensor"), None),
        P(("dp", "tensor"), None),
        P(("dp", "tensor")),
        P(),
        P(),
        P(("dp", "tensor")),
        P("dp", "tensor"),
        P("dp", "tensor"),
        P("dp", "tensor"),
        P(("dp", "tensor")),
        P(("dp", "tensor")),
        P("tensor", "dp"),
        P(("dp", "tensor")),
        P("dp", "tensor"),
        P("dp", "tensor"),
        P("tensor", "dp"),
    )
    return jax.shard_map(
        shards,
        mesh=mesh,
        in_specs=placed,
        out_specs=(
            P(("dp", "tensor"), None),
            P(("dp", "tensor"), None),
            P(("dp", "tensor")),
            P("dp", "tensor"),
            P("dp", "tensor"),
            P("dp", "tensor"),
            P(("dp", "tensor")),
            P(("dp", "tensor")),
            P("tensor", "dp"),
            P(("dp", "tensor")),
            P("dp", "tensor"),
            P("dp", "tensor"),
            P("tensor", "dp"),
            P(),
        ),
        check_vma=False,
    )
```

profile of v0, /device:TPU:0, one launch (start us, length us, event | category | flops | bytes accessed | tf_op | source)
XLA Modules:
  0.0 2123.9 jit_solution(11372836991975916970)
XLA Ops:
  11.9 42.3 %all-reduce.89 = (f32[2048]{0:T(1024)S(1)}, f32[2048]{0:T(1024)S(1)}, f32[2048]{0:T(1024)S(1)}, f32[2048]{0:T(1024)S(1)}) all-reduce(f32[2048]{0:T(1024)S(1)} %dynamic-update-slice, f32[2048]{0:T(1024)S(1)} %dynamic-update-slice.1, f32[2048]{0:T(1024)S(1)} %dynamic-update-slice.2, ...), channel_id=1, replica_groups=mesh['dp'=8,'tensor'=4] {'dp','tensor'}, use_global_device_ids=true, to_apply=%add.80 | all-reduce | flops 8192 | bytes 65536
  61.3 17.5 all-gather.16.cloned.1.call-done
  78.8 51.2 %all-gather.18.cloned.1.call-done = bf16[2048,512]{1,0:T(8,128)(2,1)} async-done(((bf16[256,512]{1,0:T(8,128)(2,1)}), bf16[2048,512]{1,0:T(8,128)(2,1)}) %all-gather.18.cloned.1.call-update) | async-done | bytes 2097168 | tf_op jit(solution)/shard_map/all_gather | solution.py:126
  134.6 45.3 %all-gather.20.cloned.1.call-done = bf16[2048,512]{1,0:T(8,128)(2,1)} async-done(((bf16[256,512]{1,0:T(8,128)(2,1)}), bf16[2048,512]{1,0:T(8,128)(2,1)}) %all-gather.20.cloned.1.call-update) | async-done | bytes 2097168 | tf_op jit(solution)/shard_map/all_gather | solution.py:127
  291.4 30.5 %all-gather.1 = f32[32,1,512]{2,1,0:T(1,128)S(1)} all-gather(f32[4,1,512]{2,1,0:T(1,128)S(1)} %slice_add_fusion.2), channel_id=3, replica_groups=mesh['dp'=8,'tensor'=4] {'dp'}, dimensions={0}, use_global_device_ids=true | all-gather | bytes 73728 | tf_op jit(solution)/shard_map/all_gather | solution.py:160
  333.7 30.5 %all-gather = f32[32,1,512]{2,1,0:T(1,128)S(1)} all-gather(f32[4,1,512]{2,1,0:T(1,128)S(1)} %slice_add_fusion.3), channel_id=2, replica_groups=mesh['dp'=8,'tensor'=4] {'dp'}, dimensions={0}, use_global_device_ids=true | all-gather | bytes 73728 | tf_op jit(solution)/shard_map/all_gather | solution.py:161
  385.1 42.7 %reduce-scatter.12.cloned.1.call-done = f32[128,2048]{1,0:T(8,128)} async-done(((f32[512,2048]{1,0:T(8,128)}), f32[128,2048]{1,0:T(8,128)}) %reduce-scatter.12.cloned.1.call-update) | async-done | bytes 1048592 | tf_op jit(solution)/shard_map/reduce_scatter | solution.py:77
  434.5 87.8 %all-gather.28.cloned.1.call-done = bf16[2048,1408]{1,0:T(8,128)(2,1)} async-done(((bf16[256,1408]{1,0:T(8,128)(2,1)}), bf16[2048,1408]{1,0:T(8,128)(2,1)}) %all-gather.28.cloned.1.call-update) | async-done | bytes 5767184 | tf_op jit(solution)/shard_map/all_gather | solution.py:130
  522.3 22.9 %all-gather.26.cloned.1.call-done = bf16[512,2048]{1,0:T(8,128)(2,1)} async-done(((bf16[128,2048]{1,0:T(8,128)(2,1)}), bf16[512,2048]{1,0:T(8,128)(2,1)}) %all-gather.26.cloned.1.call-update) | async-done | bytes 2097168 | tf_op jit(solution)/shard_map/all_gather | solution.py:73
  553.4 86.3 %all-gather.30.cloned.1.call-done = bf16[2048,1408]{1,0:T(8,128)(2,1)} async-done(((bf16[256,1408]{1,0:T(8,128)(2,1)}), bf16[2048,1408]{1,0:T(8,128)(2,1)}) %all-gather.30.cloned.1.call-update) | async-done | bytes 5767184 | tf_op jit(solution)/shard_map/all_gather | solution.py:131
  648.0 14.5 all-gather.34.cloned.1.call-done
  662.5 95.2 %all-gather.32.cloned.1.call-done = bf16[1408,2048]{1,0:T(8,128)(2,1)} async-done(((bf16[1408,256]{1,0:T(8,128)(2,1)}), bf16[1408,2048]{1,0:T(8,128)(2,1)}) %all-gather.32.cloned.1.call-update) | async-done | bytes 5767184 | tf_op jit(solution)/shard_map/all_gather | solution.py:132
  788.8 33.9 %reduce-scatter.16.cloned.1.call-done = f32[128,2048]{1,0:T(8,128)} async-done(((f32[512,2048]{1,0:T(8,128)}), f32[128,2048]{1,0:T(8,128)}) %reduce-scatter.16.cloned.1.call-update) | async-done | bytes 1048592 | tf_op jit(solution)/shard_map/reduce_scatter | solution.py:77
  822.6 47.2 %reduce-scatter.14.cloned.1.call-done = f32[128,2048]{1,0:T(8,128)} async-done(((f32[512,2048]{1,0:T(8,128)}), f32[128,2048]{1,0:T(8,128)}) %reduce-scatter.14.cloned.1.call-update) | async-done | bytes 1048592 | tf_op jit(solution)/shard_map/reduce_scatter | solution.py:77
  1017.7 30.8 %all-gather.3 = f32[32,1,512]{2,1,0:T(1,128)S(1)} all-gather(f32[4,1,512]{2,1,0:T(1,128)S(1)} %get-tuple-element.55), channel_id=5, replica_groups=mesh['dp'=8,'tensor'=4] {'dp'}, dimensions={0}, use_global_device_ids=true | all-gather | bytes 73728 | tf_op jit(solution)/shard_map/all_gather | solution.py:252
  1049.4 30.5 %all-gather.2 = f32[32,1,512]{2,1,0:T(1,128)S(1)} all-gather(f32[4,1,512]{2,1,0:T(1,128)S(1)} %get-tuple-element.56), channel_id=4, replica_groups=mesh['dp'=8,'tensor'=4] {'dp'}, dimensions={0}, use_global_device_ids=true | all-gather | bytes 73728 | tf_op jit(solution)/shard_map/all_gather | solution.py:253
  1159.1 42.8 %all-reduce.88 = (f32[2048]{0:T(1024)S(1)}, f32[2048]{0:T(1024)S(1)}, f32[2048]{0:T(1024)S(1)}, f32[2048]{0:T(1024)S(1)}, f32[1]{0:T(128)}, /*index=5*/f32[1]{0:T(128)}, f32[1]{0:T(128)}, f32[]{:T(128)}) all-reduce(f32[2048]{0:T(1024)S(1)} %get-tuple-element.18, ...), channel_id=10, replica_groups=mesh['dp'=8,'tensor'=4] {'dp','tensor'}, use_global_device_ids=true, to_apply=%region_19.20.clone | all-reduce | flops 8196 | bytes 65568
  1209.7 41.3 %reduce-scatter.20.cloned.1.call-done = f32[256,512]{1,0:T(8,128)} async-done(((f32[2048,512]{1,0:T(8,128)}), f32[256,512]{1,0:T(8,128)}) %reduce-scatter.20.cloned.1.call-update) | async-done | bytes 524304 | tf_op jit(solution)/shard_map/reduce_scatter | solution.py:279
  1251.0 92.0 %reduce-scatter.22.cloned.1.call-done = f32[256,512]{1,0:T(8,128)} async-done(((f32[2048,512]{1,0:T(8,128)}), f32[256,512]{1,0:T(8,128)}) %reduce-scatter.22.cloned.1.call-update) | async-done | bytes 524304 | tf_op jit(solution)/shard_map/reduce_scatter | solution.py:280
  1343.0 92.4 %reduce-scatter.26.cloned.1.call-done = f32[512,256]{1,0:T(8,128)} async-done(((f32[512,2048]{1,0:T(8,128)}), f32[512,256]{1,0:T(8,128)}) %reduce-scatter.26.cloned.1.call-update) | async-done | bytes 524304 | tf_op jit(solution)/shard_map/reduce_scatter | solution.py:282
  1435.4 92.2 %reduce-scatter.24.cloned.1.call-done = f32[256,512]{1,0:T(8,128)} async-done(((f32[2048,512]{1,0:T(8,128)}), f32[256,512]{1,0:T(8,128)}) %reduce-scatter.24.cloned.1.call-update) | async-done | bytes 524304 | tf_op jit(solution)/shard_map/reduce_scatter | solution.py:281
  1527.6 196.5 %reduce-scatter.28.cloned.1.call-done = f32[256,1408]{1,0:T(8,128)} async-done(((f32[2048,1408]{1,0:T(8,128)}), f32[256,1408]{1,0:T(8,128)}) %reduce-scatter.28.cloned.1.call-update) | async-done | bytes 1441808 | tf_op jit(solution)/shard_map/reduce_scatter | solution.py:283
  1724.1 196.1 %reduce-scatter.30.cloned.1.call-done = f32[256,1408]{1,0:T(8,128)} async-done(((f32[2048,1408]{1,0:T(8,128)}), f32[256,1408]{1,0:T(8,128)}) %reduce-scatter.30.cloned.1.call-update) | async-done | bytes 1441808 | tf_op jit(solution)/shard_map/reduce_scatter | solution.py:284
  1920.3 196.5 %reduce-scatter.32.cloned.1.call-done = f32[1408,256]{1,0:T(8,128)} async-done(((f32[1408,2048]{1,0:T(8,128)}), f32[1408,256]{1,0:T(8,128)}) %reduce-scatter.32.cloned.1.call-update) | async-done | bytes 1441808 | tf_op jit(solution)/shard_map/reduce_scatter | solution.py:285
  (600 shorter events, 447.9 us)
Async XLA Ops:
  7.2 71.6 %all-gather.16.cloned.1.call-start = ((), (), s32[]{:S(2)}) async-start(), calls=%async_computation.11 | async-start | bytes 2621440 | tf_op jit(solution)/shard_map/all_gather | solution.py:73
  8.5 126.1 %copy-start.55 = (f32[128]{0:T(128)}, f32[128]{0:T(128)S(1)}, u32[]{:S(2)}) copy-start(f32[128]{0:T(128)S(1)} %add_rsqrt_fusion.2) | copy-start | bytes 1540
  56.3 73.8 %all-gather.18.cloned.1.call-start = ((), (), s32[]{:S(2)}) async-start(), calls=%async_computation.12 | async-start | bytes 2359296 | tf_op jit(solution)/shard_map/all_gather | solution.py:126
  57.0 122.8 %all-gather.20.cloned.1.call-start = ((), (), s32[]{:S(2)}) async-start(), calls=%async_computation.13 | async-start | bytes 2359296 | tf_op jit(solution)/shard_map/all_gather | solution.py:127
  57.8 317.3 %all-gather.22.cloned.1.call-start = ((), (), s32[]{:S(2)}) async-start(), calls=%async_computation.14 | async-start | bytes 2359296 | tf_op jit(solution)/shard_map/all_gather | solution.py:128
  58.4 320.8 %all-gather.24.cloned.1.call-start = ((), (), s32[]{:S(2)}) async-start(), calls=%async_computation.15 | async-start | bytes 2359296 | tf_op jit(solution)/shard_map/all_gather | solution.py:129
  58.9 368.8 %reduce-scatter.12.cloned.1.call-start = ((), (), s32[]{:S(2)}) async-start(), calls=%async_computation.16 | async-start | bytes 5242880 | tf_op jit(solution)/shard_map/reduce_scatter | solution.py:77
  60.0 119.9 %copy-start.52 = (f32[512]{0:T(512)}, f32[512]{0:T(512)S(1)}, u32[]{:S(2)}) copy-start(f32[512]{0:T(512)S(1)} %select_bitcast_fusion) | copy-start | bytes 6148
  384.3 138.0 %all-gather.28.cloned.1.call-start = ((), (), s32[]{:S(2)}) async-start(), calls=%async_computation.18 | async-start | bytes 6488064 | tf_op jit(solution)/shard_map/all_gather | solution.py:130
  385.1 160.1 %all-gather.26.cloned.1.call-start = ((), (), s32[]{:S(2)}) async-start(), calls=%async_computation.17 | async-start | bytes 2621440 | tf_op jit(solution)/shard_map/all_gather | solution.py:73
  430.9 208.8 %all-gather.30.cloned.1.call-start = ((), (), s32[]{:S(2)}) async-start(), calls=%async_computation.19 | async-start | bytes 6488064 | tf_op jit(solution)/shard_map/all_gather | solution.py:131
  431.6 230.8 %all-gather.34.cloned.1.call-start = ((), (), s32[]{:S(2)}) async-start(), calls=%async_computation.22 | async-start | bytes 2621440 | tf_op jit(solution)/shard_map/all_gather | solution.py:73
  433.7 324.0 %all-gather.32.cloned.1.call-start = ((), (), s32[]{:S(2)}) async-start(), calls=%async_computation.20 | async-start | bytes 6488064 | tf_op jit(solution)/shard_map/all_gather | solution.py:132
  434.5 388.2 %reduce-scatter.16.cloned.1.call-start = ((), (), s32[]{:S(2)}) async-start(), calls=%async_computation.23 | async-start | bytes 5242880 | tf_op jit(solution)/shard_map/reduce_scatter | solution.py:77
  779.7 90.1 %reduce-scatter.14.cloned.1.call-start = ((), (), s32[]{:S(2)}) async-start(), calls=%async_computation.21 | async-start | bytes 5242880 | tf_op jit(solution)/shard_map/reduce_scatter | solution.py:77
  788.3 109.2 %all-gather.36.cloned.1.call-start = ((), (), s32[]{:S(2)}) async-start(), calls=%async_computation.24 | async-start | bytes 2621440 | tf_op jit(solution)/shard_map/all_gather | solution.py:73
  874.8 282.7 %reduce-scatter.18.cloned.1.call-start = ((), (), s32[]{:S(2)}) async-start(), calls=%async_computation.25 | async-start | bytes 5242880 | tf_op jit(solution)/shard_map/reduce_scatter | solution.py:77
  1111.9 139.1 %reduce-scatter.20.cloned.1.call-start = ((), (), s32[]{:S(2)}) async-start(), calls=%async_computation.26 | async-start | bytes 4718592 | tf_op jit(solution)/shard_map/reduce_scatter | solution.py:279
  1115.2 227.8 %reduce-scatter.22.cloned.1.call-start = ((), (), s32[]{:S(2)}) async-start(), calls=%async_computation.27 | async-start | bytes 4718592 | tf_op jit(solution)/shard_map/reduce_scatter | solution.py:280
  1118.7 316.7 %reduce-scatter.26.cloned.1.call-start = ((), (), s32[]{:S(2)}) async-start(), calls=%async_computation.29 | async-start | bytes 4718592 | tf_op jit(solution)/shard_map/reduce_scatter | solution.py:282
  1125.2 402.4 %reduce-scatter.24.cloned.1.call-start = ((), (), s32[]{:S(2)}) async-start(), calls=%async_computation.28 | async-start | bytes 4718592 | tf_op jit(solution)/shard_map/reduce_scatter | solution.py:281
  1129.5 594.6 %reduce-scatter.28.cloned.1.call-start = ((), (), s32[]{:S(2)}) async-start(), calls=%async_computation.30 | async-start | bytes 12976128 | tf_op jit(solution)/shard_map/reduce_scatter | solution.py:283
  1138.9 781.4 %reduce-scatter.30.cloned.1.call-start = ((), (), s32[]{:S(2)}) async-start(), calls=%async_computation.31 | async-start | bytes 12976128 | tf_op jit(solution)/shard_map/reduce_scatter | solution.py:284
  1146.7 970.1 %reduce-scatter.32.cloned.1.call-start = ((), (), s32[]{:S(2)}) async-start(), calls=%async_computation.32 | async-start | bytes 12976128 | tf_op jit(solution)/shard_map/reduce_scatter | solution.py:285
  (68 other events, 787.9 us)
Sparse Core Ops, SparseCore 0:
  56.4 22.3 all-gather.15
  80.9 49.0 all-gather.17
  132.2 47.6 all-gather.19
  181.8 47.6 all-gather.21
  231.4 48.8 all-gather.23
  384.4 43.2 reduce-scatter.11
  429.9 92.2 all-gather.27
  524.4 20.7 all-gather.25
  547.4 92.3 all-gather.29
  641.7 20.7 all-gather.33
  664.5 93.1 all-gather.31
  779.9 42.7 reduce-scatter.15
  825.2 44.5 reduce-scatter.13
  874.9 22.5 all-gather.35
  1112.0 45.3 reduce-scatter.17
  1161.5 89.4 reduce-scatter.19
  1255.0 87.9 reduce-scatter.21
  1347.1 88.3 reduce-scatter.25
  1439.6 87.9 reduce-scatter.23
  1531.6 192.4 reduce-scatter.27
  1728.3 191.9 reduce-scatter.29
  1924.4 192.3 reduce-scatter.31
where the time goes:
time: 2140 us; the launch traced here: 2120 us
  waiting for transfers between devices  1460 us (68%)
  local copies, waits for them, and re-layouts  219 us (10%)
  blocking collectives  219 us (10%)
  matrix products  115 us (5%)
  other arithmetic  91.4 us (4%)
    reduce_scatter x1, waiting for transfers between devices, shards(): lax.psum_scatter(grad_down, 'dp', scatter_dimension=1, tiled=True)  197 us
    reduce_scatter x1, waiting for transfers between devices, shards(): lax.psum_scatter(grad_gate, 'dp', scatter_dimension=0, tiled=True)  197 us
    reduce_scatter x1, waiting for transfers between devices, shards(): lax.psum_scatter(grad_up, 'dp', scatter_dimension=0, tiled=True)  196 us
    reduce_scatter x4, waiting for transfers between devices, tensor_reduce(): lax.psum_scatter(partial_term(jnp.int32(0), row_count * lax.axis_size('te...  124 us
    all_gather x1, waiting for transfers between devices, shards(): lax.all_gather(w_down, 'dp', axis=1, tiled=True)  95.2 us
    reduce_scatter x1, waiting for transfers between devices, shards(): lax.psum_scatter(grad_wout, 'dp', scatter_dimension=1, tiled=True)  92.4 us
    reduce_scatter x1, waiting for transfers between devices, shards(): lax.psum_scatter(grad_wmix, 'dp', scatter_dimension=0, tiled=True)  92.2 us
    reduce_scatter x1, waiting for transfers between devices, shards(): lax.psum_scatter(grad_wforget, 'dp', scatter_dimension=0, tiled=True)  92 us
  transfers between devices with their start and end apart: 22, of which 20 were waited for; matrix products, arithmetic and copies ran while one was open for 11% of the time, Pallas kernels for 0%

commit v1 on v0

v1 whole, which is shorter than its diff:
```python
import functools

import jax
import jax.numpy as jnp
from jax import lax
from jax.experimental import pallas as pl
from jax.experimental.pallas import tpu as pltpu
from jax.sharding import PartitionSpec as P

D = 2048
BLOCK = 128
MESH = pl.DeviceIdType.MESH

epsilon = 1e-06
lower_bound = 0.75
TILE = 8


def row_scale(values):
    return lax.rsqrt(jnp.mean(values * values, axis=1, keepdims=True) + epsilon)


def dot(operand, matrix):
    return jnp.dot(operand, matrix, preferred_element_type=jnp.float32)


def times_transposed(operand, matrix):
    return lax.dot_general(
        operand, matrix, (((1,), (1,)), ((), ())), preferred_element_type=jnp.float32
    )


def inner_rows(operand, matrix):
    return lax.dot_general(
        operand, matrix, (((0,), (0,)), ((), ())), preferred_element_type=jnp.float32
    )


def silu_slope(values, sigmoid_value):
    return sigmoid_value * (1.0 + values * (1.0 - sigmoid_value))


def norm_back(grad_normed, scaled_rows, row_factor, gain_vector):
    grad_scaled = grad_normed * gain_vector
    mean_term = jnp.mean(grad_scaled * scaled_rows, axis=1, keepdims=True)
    return (
        row_factor * (grad_scaled - scaled_rows * mean_term),
        jnp.sum(grad_normed * scaled_rows, axis=0),
    )


def widen(values, channel_start):
    return lax.dynamic_update_slice_in_dim(jnp.zeros((D,), jnp.float32), values, channel_start, 0)


def tensor_rows(values):
    return lax.all_gather(values, "tensor", axis=0, tiled=True)


def tensor_reduce(partial_term):
    return lax.psum_scatter(
        partial_term.astype(jnp.bfloat16), "tensor", scatter_dimension=0, tiled=True
    ).astype(jnp.float32)


def flat_exchange_kernel(dp, tp, reduce, x_ref, out_ref, held, send_sem, recv_sem):
    count = dp * tp
    me = lax.axis_index("dp") * tp + lax.axis_index("tensor")
    barrier = pltpu.get_barrier_semaphore()

    def place(k):
        peer = lax.rem(me + k, count)
        return peer, (lax.div(peer, tp), lax.rem(peer, tp))

    def greet(k, carry):
        _, where = place(k)
        pl.semaphore_signal(barrier, inc=1, device_id=where, device_id_type=MESH)
        return carry

    lax.fori_loop(1, count, greet, 0)
    held[pl.ds(me, 1)] = x_ref[pl.ds(me if reduce else 0, 1)]
    pl.semaphore_wait(barrier, count - 1)

    def send(k, carry):
        peer, where = place(k)
        pltpu.make_async_remote_copy(
            src_ref=x_ref.at[pl.ds(peer if reduce else 0, 1)],
            dst_ref=held.at[pl.ds(me, 1)],
            send_sem=send_sem,
            recv_sem=recv_sem,
            device_id=where,
            device_id_type=MESH,
        ).start()
        return carry

    lax.fori_loop(1, count, send, 0)
    rows = held.at[pl.ds(0, count - 1)]
    pltpu.make_async_copy(rows, rows, send_sem).wait()
    pltpu.make_async_copy(rows, rows, recv_sem).wait()
    if reduce:
        out_ref[...] = jnp.sum(held[...], axis=0, keepdims=True)
    else:
        out_ref[...] = held[...]


def flat_exchange(x, dp, tp, reduce):
    count = dp * tp
    return pl.pallas_call(
        functools.partial(flat_exchange_kernel, dp, tp, reduce),
        out_shape=jax.ShapeDtypeStruct((1 if reduce else count, 8, 128), jnp.float32),
        in_specs=[pl.BlockSpec(memory_space=pltpu.VMEM)],
        out_specs=pl.BlockSpec(memory_space=pltpu.VMEM),
        scratch_shapes=[
            pltpu.VMEM((count, 8, 128), jnp.float32),
            pltpu.SemaphoreType.DMA,
            pltpu.SemaphoreType.DMA,
        ],
        compiler_params=pltpu.CompilerParams(
            collective_id=1 if reduce else 0, has_side_effects=True
        ),
        cost_estimate=pl.CostEstimate(flops=0, bytes_accessed=16 << 20, transcendentals=0),
        name="flat_reduce" if reduce else "flat_gather",
    )(x)


def carry_kernel(dp, reverse, ends_ref, rows_ref, ids_ref, out_ref, held, entering, send_sem, recv_sem):
    me = lax.axis_index("dp")
    barrier = pltpu.get_barrier_semaphore()
    height = ends_ref.shape[0]
    here = height // 2
    blocks = rows_ref.shape[0]

    def greet(k, carry):
        pl.semaphore_signal(
            barrier, inc=1, device_id={"dp": lax.rem(me + k, dp)}, device_id_type=MESH
        )
        return carry

    lax.fori_loop(1, dp, greet, 0)
    own = pl.ds(pl.multiple_of(me * height, height), height)
    held[own, :] = ends_ref[...]
    pl.semaphore_wait(barrier, dp - 1)

    def send(k, carry):
        pltpu.make_async_remote_copy(
            src_ref=ends_ref,
            dst_ref=held.at[own],
            send_sem=send_sem,
            recv_sem=recv_sem,
            device_id={"dp": lax.rem(me + k, dp)},
            device_id_type=MESH,
        ).start()
        return carry

    lax.fori_loop(1, dp, send, 0)
    rows = held.at[pl.ds(0, (dp - 1) * height)]
    pltpu.make_async_copy(rows, rows, send_sem).wait()
    pltpu.make_async_copy(rows, rows, recv_sem).wait()

    def step(i, state):
        p = blocks - 1 - i if reverse else i
        entering[pl.ds(p, 1), :] = state
        row = rows_ref[p]
        return held[pl.ds(row, 1), :] * state + held[pl.ds(row + here, 1), :]

    lax.fori_loop(0, blocks, step, jnp.zeros((1, ends_ref.shape[1]), jnp.float32))
    for b in range(here):
        out_ref[pl.ds(b, 1), :] = entering[pl.ds(ids_ref[b], 1), :]


def block_carry(ends, pack_rows, block_ids, dp, reverse):
    height, width = ends.shape
    blocks = pack_rows.shape[0]
    return pl.pallas_call(
        functools.partial(carry_kernel, dp, reverse),
        out_shape=jax.ShapeDtypeStruct((height // 2, width), jnp.float32),
        in_specs=[
            pl.BlockSpec(memory_space=pltpu.VMEM),
            pl.BlockSpec(memory_space=pltpu.SMEM),
            pl.BlockSpec(memory_space=pltpu.SMEM),
        ],
        out_specs=pl.BlockSpec(memory_space=pltpu.VMEM),
        scratch_shapes=[
            pltpu.VMEM((dp * height, width), jnp.float32),
            pltpu.VMEM((blocks, width), jnp.float32),
            pltpu.SemaphoreType.DMA,
            pltpu.SemaphoreType.DMA,
        ],
        compiler_params=pltpu.CompilerParams(
            collective_id=3 if reverse else 2, has_side_effects=True
        ),
        cost_estimate=pl.CostEstimate(flops=0, bytes_accessed=16 << 20, transcendentals=0),
        name="carry_back" if reverse else "carry_fwd",
    )(ends, pack_rows, block_ids)


def scan_kernel(input_ref, forget_ref, bias_ref, keep_ref, cum_ref, local_ref, ends_ref):
    width = input_ref.shape[1]
    here = input_ref.shape[0] // BLOCK
    line = lax.broadcasted_iota(jnp.int32, (TILE, width), 0)

    def tile_step(i, carry):
        out = []
        for b in range(here):
            rows = pl.ds(pl.multiple_of(b * BLOCK + i * TILE, TILE), TILE)
            forget = lower_bound + (1.0 - lower_bound) * lax.logistic(forget_ref[rows, :] + bias_ref[...])
            raw = input_ref[rows, :]
            total = raw * lax.logistic(raw) * (1.0 - forget)
            decay = forget * keep_ref[rows, :]
            for shift in (1, 2, 4):
                ahead = line >= shift
                before_total = pltpu.roll(total, shift, 0)
                before_decay = pltpu.roll(decay, shift, 0)
                total = jnp.where(ahead, decay * before_total + total, total)
                decay = jnp.where(ahead, decay * before_decay, decay)
            far_decay, far_total = carry[2 * b], carry[2 * b + 1]
            total = decay * far_total + total
            decay = decay * far_decay
            cum_ref[rows, :] = decay
            local_ref[rows, :] = total
            out += [decay[TILE - 1 :, :], total[TILE - 1 :, :]]
        return tuple(out)

    start = (jnp.ones((1, width), jnp.float32), jnp.zeros((1, width), jnp.float32)) * here
    last = lax.fori_loop(0, BLOCK // TILE, tile_step, start)
    for b in range(here):
        ends_ref[pl.ds(b, 1), :] = last[2 * b]
        ends_ref[pl.ds(here + b, 1), :] = last[2 * b + 1]


def local_scan(input_raw, forget_raw, bias, keep):
    rows, width = input_raw.shape
    full = jax.ShapeDtypeStruct((rows, width), jnp.float32)
    return pl.pallas_call(
        scan_kernel,
        out_shape=(full, full, jax.ShapeDtypeStruct((2 * (rows // BLOCK), width), jnp.float32)),
        in_specs=[pl.BlockSpec(memory_space=pltpu.VMEM)] * 4,
        out_specs=(pl.BlockSpec(memory_space=pltpu.VMEM),) * 3,
        cost_estimate=pl.CostEstimate(flops=0, bytes_accessed=12 << 20, transcendentals=0),
        name="scan_fwd",
    )(input_raw, forget_raw, bias, keep)


def scan_back_kernel(grad_ref, forget_ref, bias_ref, keep_ref, decay_ref, total_ref, ends_ref):
    width = grad_ref.shape[1]
    here = grad_ref.shape[0] // BLOCK
    tiles = BLOCK // TILE
    line = lax.broadcasted_iota(jnp.int32, (TILE, width), 0)

    def tile_step(i, carry):
        out = []
        for b in range(here):
            rows = pl.ds(pl.multiple_of(b * BLOCK + (tiles - 1 - i) * TILE, TILE), TILE)
            forget = lower_bound + (1.0 - lower_bound) * lax.logistic(forget_ref[rows, :] + bias_ref[...])
            own_decay = forget * keep_ref[rows, :]
            next_decay, far_decay, far_total = carry[3 * b : 3 * b + 3]
            decay = jnp.where(line == TILE - 1, next_decay, pltpu.roll(own_decay, TILE - 1, 0))
            total = grad_ref[rows, :]
            for shift in (1, 2, 4):
                behind = line < TILE - shift
                after_total = pltpu.roll(total, TILE - shift, 0)
                after_decay = pltpu.roll(decay, TILE - shift, 0)
                total = jnp.where(behind, decay * after_total + total, total)
                decay = jnp.where(behind, decay * after_decay, decay)
            total = decay * far_total + total
            decay = decay * far_decay
            decay_ref[rows, :] = decay
            total_ref[rows, :] = total
            out += [own_decay[:1, :], decay[:1, :], total[:1, :]]
        return tuple(out)

    one = jnp.ones((1, width), jnp.float32)
    last = lax.fori_loop(0, tiles, tile_step, (one, one, jnp.zeros_like(one)) * here)
    for b in range(here):
        ends_ref[pl.ds(b, 1), :] = last[3 * b] * last[3 * b + 1]
        ends_ref[pl.ds(here + b, 1), :] = last[3 * b] * last[3 * b + 2]


def local_scan_back(grad_direct, forget_raw, bias, keep):
    rows, width = grad_direct.shape
    full = jax.ShapeDtypeStruct((rows, width), jnp.float32)
    return pl.pallas_call(
        scan_back_kernel,
        out_shape=(full, full, jax.ShapeDtypeStruct((2 * (rows // BLOCK), width), jnp.float32)),
        in_specs=[pl.BlockSpec(memory_space=pltpu.VMEM)] * 4,
        out_specs=(pl.BlockSpec(memory_space=pltpu.VMEM),) * 3,
        cost_estimate=pl.CostEstimate(flops=0, bytes_accessed=12 << 20, transcendentals=0),
        name="scan_back",
    )(grad_direct, forget_raw, bias, keep)


def gate_back_kernel(
    decay_ref, total_ref, back_ref, cum_ref, local_ref, carry_ref, input_ref, forget_ref, bias_ref, keep_ref,
    grad_input_ref, grad_forget_ref, grad_bias_ref,
):
    b = pl.program_id(0)
    state_grad = total_ref[...] + decay_ref[...] * back_ref[pl.ds(b, 1), :]
    entering = carry_ref[pl.ds(b, 1), :]
    hidden = local_ref[...] + cum_ref[...] * entering
    line = lax.broadcasted_iota(jnp.int32, hidden.shape, 0)
    before = jnp.where(line == 0, entering, pltpu.roll(hidden, 1, 0))
    sigma = lax.logistic(forget_ref[...] + bias_ref[...])
    forget = lower_bound + (1.0 - lower_bound) * sigma
    raw = input_ref[...]
    input_sigma = lax.logistic(raw)
    grad_forget = keep_ref[...] * state_grad * before - state_grad * (raw * input_sigma)
    grad_pre = grad_forget * (1.0 - lower_bound) * sigma * (1.0 - sigma)
    grad_forget_ref[...] = grad_pre.astype(jnp.bfloat16)
    grad_input_ref[...] = (state_grad * (1.0 - forget) * silu_slope(raw, input_sigma)).astype(jnp.bfloat16)

    @pl.when(b == 0)
    def _():
        grad_bias_ref[...] = jnp.zeros_like(grad_bias_ref)

    grad_bias_ref[...] += jnp.sum(grad_pre, axis=0, keepdims=True)


def gate_back(tail_decay, tail_grad, carry_back, cum, local, carry_in, input_raw, forget_raw, bias, keep):
    rows, width = input_raw.shape
    here = rows // BLOCK
    tall = pl.BlockSpec((BLOCK, width), lambda b: (b, 0))
    small = pl.BlockSpec((here, width), lambda b: (0, 0))
    line = pl.BlockSpec((1, width), lambda b: (0, 0))
    half = jax.ShapeDtypeStruct((rows, width), jnp.bfloat16)
    return pl.pallas_call(
        gate_back_kernel,
        grid=(here,),
        out_shape=(half, half, jax.ShapeDtypeStruct((1, width), jnp.float32)),
        in_specs=[tall, tall, small, tall, tall, small, tall, tall, line, pl.BlockSpec((BLOCK, 1), lambda b: (b, 0))],
        out_specs=(tall, tall, line),
        cost_estimate=pl.CostEstimate(flops=0, bytes_accessed=12 << 20, transcendentals=0),
        name="gate_back",
    )(tail_decay, tail_grad, carry_back, cum, local, carry_in, input_raw, forget_raw, bias, keep)


class Plain:
    def __init__(self, dp):
        self.dp = dp

    def to_slots(self, values):
        return values

    def from_slots(self, values):
        return values

    def gather(self, shard, mode):
        return (lax.all_gather(shard, "dp", axis=0, tiled=True),)

    def reduce(self, rows, cols, mode):
        partial_sum = inner_rows(rows[0], cols).astype(jnp.bfloat16)
        return lax.psum_scatter(partial_sum, "dp", scatter_dimension=0, tiled=True).astype(jnp.float32)

    def split(self, values):
        return (values,)


class Chain:
    def __init__(self, dp, window=2):
        self.dp = dp
        self.length = dp // 2
        index = lax.axis_index("dp")
        self.pos = lax.div(index, 2)
        self.pair = lax.rem(index, 2)
        self.block = D // dp
        self.window = window
        self.history = {"up": [], "down": [], "pair": []}

    def send(self, lane, values, pairs):
        past = self.history[lane]
        if len(past) >= self.window:
            values, _ = lax.optimization_barrier((values, past[-self.window]))
        arrived = lax.ppermute(values, "dp", pairs)
        past.append(arrived)
        return arrived

    def up(self, values, first, last):
        return self.send("up", values, [(2 * z + y, 2 * z + 2 + y) for z in range(first, last + 1) for y in range(2)])

    def down(self, values, first, last):
        return self.send("down", values, [(2 * z + y, 2 * z - 2 + y) for z in range(first, last + 1) for y in range(2)])

    def swap(self, values):
        return self.send("pair", values, [(i, i ^ 1) for i in range(self.dp)])

    def to_slots(self, values):
        places = []
        for other in range(2):
            for r in range(self.length):
                start = (lax.rem(self.pos + self.length - r, self.length) * 2 + (self.pair ^ other)) * self.block
                places.append(lax.dynamic_slice_in_dim(values, start, self.block, values.ndim - 1))
        return jnp.concatenate(places, axis=-1)

    def from_slots(self, values):
        places = []
        for z in range(self.length):
            for y in range(2):
                start = ((self.pair ^ y) * self.length + lax.rem(self.pos + self.length - z, self.length)) * self.block
                places.append(lax.dynamic_slice_in_dim(values, start, self.block, values.ndim - 1))
        return jnp.concatenate(places, axis=-1)

    def spread(self, piece):
        n = self.length
        ups, downs = [piece], [piece]
        for r in range(1, n):
            ups.append(self.up(ups[-1], r - 1, n - 2))
            downs.append(self.down(downs[-1], 1, n - r))
        return [piece] + [jnp.where(self.pos >= r, ups[r], downs[n - r]) for r in range(1, n)]

    def collect(self, slots):
        n = self.length
        term = lambda r, arrived: (slots[r] + arrived.astype(jnp.float32)).astype(jnp.bfloat16)
        up, down = slots[1].astype(jnp.bfloat16), slots[n - 1].astype(jnp.bfloat16)
        for k in range(1, n):
            up_in = self.up(up, 0, min(k - 1, n - 2))
            down_in = self.down(down, max(n - k, 1), n - 1)
            if k < n - 1:
                up, down = term(k + 1, up_in), term(n - 1 - k, down_in)
        return slots[0] + up_in.astype(jnp.float32) + down_in.astype(jnp.float32)

    def gather(self, shard, mode):
        rows = shard.shape[0]
        if mode == "chain first":
            own = jnp.concatenate(self.spread(shard), axis=0)
            return own, self.swap(own)
        both = jnp.stack([shard, self.swap(shard)])
        slots = self.spread(both)
        return (
            jnp.concatenate([s[0] for s in slots], axis=0),
            jnp.concatenate([s[1] for s in slots], axis=0),
        )

    def reduce(self, rows, cols, mode):
        own_rows, other_rows = rows
        n, size = self.length, self.block
        other = inner_rows(other_rows, cols).astype(jnp.bfloat16)
        if mode == "chain first":
            own = inner_rows(own_rows, cols).astype(jnp.bfloat16)
            halves = [v.reshape(n, 1, size, -1) for v in (own, other)]
            both = [jnp.concatenate([h[r] for h in halves], axis=0).astype(jnp.float32) for r in range(n)]
            total = self.collect(both)
            return total[0] + self.swap(total[1].astype(jnp.bfloat16)).astype(jnp.float32)
        arrived = self.swap(other).reshape(n, size, -1)
        own = inner_rows(own_rows, cols).astype(jnp.bfloat16).reshape(n, size, -1)
        return self.collect([own[r].astype(jnp.float32) + arrived[r].astype(jnp.float32) for r in range(n)])

    def split(self, values):
        return values[:, : D // 2], values[:, D // 2 :]


def across(operand_parts, weight_parts):
    total = dot(operand_parts[0], weight_parts[0])
    for operand, weight in zip(operand_parts[1:], weight_parts[1:]):
        total = total + dot(operand, weight)
    return total


def back_across(terms):
    count = len(terms[0][1])
    columns = []
    for i in range(count):
        total = times_transposed(terms[0][0], terms[0][1][i])
        for operand, parts in terms[1:]:
            total = total + times_transposed(operand, parts[i])
        columns.append(total.astype(jnp.bfloat16))
    return columns[0] if count == 1 else jnp.concatenate(columns, axis=1)


def shards(
    dp,
    tp,
    tokens,
    cotangent,
    valid_mask,
    seq_lengths,
    block_order,
    norm_gain1,
    w_input,
    w_forget,
    w_gate_mix,
    forget_bias,
    out_gain,
    w_out,
    norm_gain2,
    w_gate,
    w_up,
    w_down,
):
    count = dp * tp
    dp_index = lax.axis_index("dp")
    tensor_index = lax.axis_index("tensor")
    own_rows = tokens.shape[0]
    group_rows = own_rows * tp
    blocks_here = group_rows // BLOCK
    width_local = w_input.shape[1]
    channel_start = tensor_index * width_local
    lanes = Chain(dp) if dp == 8 else Plain(dp)

    small_width = norm_gain1.shape[0]
    packed = jnp.concatenate([norm_gain1, forget_bias, out_gain, norm_gain2])
    packed = jnp.pad(packed, (0, 1024 - packed.shape[0])).reshape(1, 8, 128)
    gathered = flat_exchange(packed, dp, tp, False).reshape(count, 1024)[:, : 4 * small_width]
    gathered = gathered.reshape(count, 4, small_width)
    gain_first = lanes.to_slots(gathered[:, 0].reshape(1, D))
    bias_local = lax.dynamic_slice_in_dim(gathered[:, 1].reshape(1, D), channel_start, width_local, 1)
    gain_out = lax.dynamic_slice_in_dim(gathered[:, 2].reshape(1, D), channel_start, width_local, 1)
    gain_second = lanes.to_slots(gathered[:, 3].reshape(1, D))

    mixer_cat = jnp.concatenate([w_input, w_forget, w_gate_mix], axis=1)
    mixer_parts = lanes.gather(mixer_cat, "chain first")
    out_parts = lanes.gather(w_out.T, "chain first")
    gate_parts = lanes.gather(w_gate, "chain first")
    up_parts = lanes.gather(w_up, "chain first")
    down_parts = lanes.gather(w_down.T, "pair first")

    block_ids = lax.dynamic_slice_in_dim(block_order, dp_index * blocks_here, blocks_here)
    positions = block_ids[:, None] * BLOCK + jnp.arange(BLOCK, dtype=jnp.int32)[None, :]
    seq_starts = jnp.cumsum(seq_lengths) - seq_lengths
    is_start = jnp.any(positions[:, :, None] == seq_starts[None, None, :], axis=2)
    keep_flag = jnp.where(is_start, 0.0, 1.0).astype(jnp.float32).reshape(group_rows, 1)
    every = jnp.arange(block_order.shape[0], dtype=jnp.int32)
    dealt = jnp.sum(jnp.where(block_order[None, :] == every[:, None], every[None, :], 0), axis=1)
    pack_rows = dealt + (dealt // blocks_here) * blocks_here

    stream = lanes.to_slots(tokens).astype(jnp.float32)
    scale_first = row_scale(stream)
    scaled_first = stream * scale_first
    mixer_in = tensor_rows((scaled_first * gain_first).astype(jnp.bfloat16))
    mixer_in_parts = lanes.split(mixer_in)
    mixer_raw = [
        across(mixer_in_parts, [p[:, i * width_local : (i + 1) * width_local] for p in mixer_parts])
        for i in range(3)
    ]
    input_raw, forget_raw, gate_raw = mixer_raw
    cum_decay, local_state, ends = local_scan(input_raw, forget_raw, bias_local, keep_flag)
    carry_in = block_carry(ends, pack_rows, block_ids, dp, False)

    def blocks(values):
        return values.reshape(blocks_here, BLOCK, width_local)

    hidden_state = (blocks(local_state) + blocks(cum_decay) * carry_in[:, None, :]).reshape(group_rows, width_local)
    square_total = lax.psum(jnp.sum(hidden_state * hidden_state, axis=1), "tensor")
    state_scale = lax.rsqrt(square_total / D + epsilon)[:, None]
    state_normed = hidden_state * state_scale
    gate_sigma = jax.nn.sigmoid(gate_raw)
    gate_act = gate_raw * gate_sigma
    mixer_cast = (state_normed * gain_out * gate_act).astype(jnp.bfloat16)
    mixer_out = tensor_reduce(back_across([(mixer_cast, out_parts)]))
    after_mixer = stream + mixer_out

    scale_second = row_scale(after_mixer)
    scaled_second = after_mixer * scale_second
    ffn_in = tensor_rows((scaled_second * gain_second).astype(jnp.bfloat16))
    ffn_in_parts = lanes.split(ffn_in)
    gate_pre = across(ffn_in_parts, gate_parts)
    up_pre = across(ffn_in_parts, up_parts)
    gate_sig = jax.nn.sigmoid(gate_pre)
    hidden_units = (gate_pre * gate_sig * up_pre).astype(jnp.bfloat16)

    valid_rows = valid_mask.astype(jnp.float32)
    grad_out = lanes.to_slots(cotangent).astype(jnp.float32) * valid_rows[:, None]
    grad_ffn_all = tensor_rows(grad_out.astype(jnp.bfloat16))
    grad_ffn_parts = lanes.split(grad_ffn_all)
    grad_down = lanes.reduce(grad_ffn_parts, hidden_units, "pair first")
    grad_hidden = across(grad_ffn_parts, down_parts)
    grad_gate_pre = (grad_hidden * up_pre * silu_slope(gate_pre, gate_sig)).astype(jnp.bfloat16)
    grad_up_pre = (grad_hidden * gate_pre * gate_sig).astype(jnp.bfloat16)
    grad_gate = lanes.reduce(ffn_in_parts, grad_gate_pre, "pair first")
    grad_up = lanes.reduce(ffn_in_parts, grad_up_pre, "pair first")
    grad_normed_second = tensor_reduce(back_across([(grad_gate_pre, gate_parts), (grad_up_pre, up_parts)]))
    ffn_out = tensor_reduce(back_across([(hidden_units, down_parts)]))
    residual_sum = after_mixer + ffn_out
    grad_stream_second, grad_gain_second = norm_back(
        grad_normed_second, scaled_second, scale_second, gain_second
    )
    grad_after = grad_out + grad_stream_second

    grad_mix_all = tensor_rows(grad_after.astype(jnp.bfloat16))
    grad_mix_parts = lanes.split(grad_mix_all)
    grad_mixed = across(grad_mix_parts, out_parts)
    grad_wout = lanes.reduce(grad_mix_parts, mixer_cast, "pair first")
    grad_gain_out_local = jnp.sum(grad_mixed * state_normed * gate_act, axis=0)
    grad_gate_raw = (
        grad_mixed * state_normed * gain_out * silu_slope(gate_raw, gate_sigma)
    ).astype(jnp.bfloat16)
    grad_normed_state = grad_mixed * gain_out * gate_act
    cross_total = lax.psum(jnp.sum(grad_normed_state * state_normed, axis=1), "tensor")
    grad_direct = state_scale * (grad_normed_state - state_normed * (cross_total / D)[:, None])
    tail_decay, tail_grad, head = local_scan_back(grad_direct, forget_raw, bias_local, keep_flag)
    carry_back = block_carry(head, pack_rows, block_ids, dp, True)
    grad_input_raw, grad_forget_raw, grad_bias_local = gate_back(
        tail_decay, tail_grad, carry_back, cum_decay, local_state, carry_in, input_raw, forget_raw, bias_local, keep_flag
    )
    grad_wmix = lanes.reduce(mixer_in_parts, grad_gate_raw, "pair first")
    grad_winput = lanes.reduce(mixer_in_parts, grad_input_raw, "pair first")
    grad_wforget = lanes.reduce(mixer_in_parts, grad_forget_raw, "pair first")
    mixer_back = [
        (g, [p[:, i * width_local : (i + 1) * width_local] for p in mixer_parts])
        for i, g in enumerate((grad_input_raw, grad_forget_raw, grad_gate_raw))
    ]
    grad_normed_first = tensor_reduce(back_across(mixer_back))
    grad_stream_first, grad_gain_first = norm_back(
        grad_normed_first, scaled_first, scale_first, gain_first
    )
    input_grad = lanes.from_slots((grad_after + grad_stream_first).astype(jnp.bfloat16))
    layer_out = lanes.from_slots(residual_sum.astype(jnp.bfloat16))

    totals = jnp.stack(
        [
            jnp.sum(valid_rows * jnp.sum(residual_sum * residual_sum, axis=1)),
            jnp.sum(valid_rows * jnp.sum(mixer_out * mixer_out, axis=1)),
            jnp.sum(valid_rows * jnp.sum(ffn_out * ffn_out, axis=1)),
            jnp.sum(valid_rows),
        ]
    )
    small_terms = [
        lanes.from_slots(grad_gain_first.reshape(1, D)),
        widen(grad_bias_local[0], channel_start),
        widen(grad_gain_out_local, channel_start),
        lanes.from_slots(grad_gain_second.reshape(1, D)),
    ]
    outgoing = jnp.concatenate(
        [term.reshape(count, small_width) for term in small_terms]
        + [jnp.broadcast_to(totals[None, :], (count, 4)), jnp.zeros((count, 1020 - 4 * small_width), jnp.float32)],
        axis=1,
    )
    summed = flat_exchange(outgoing.reshape(count, 8, 128), dp, tp, True).reshape(1024)
    small_summed = summed[: 4 * small_width].reshape(4, small_width)
    totals = summed[4 * small_width : 4 * small_width + 4]
    rms_stats = jnp.sqrt(totals[:3] / (jnp.maximum(totals[3], 1.0) * D))
    return (
        layer_out,
        input_grad,
        small_summed[0],
        grad_winput,
        grad_wforget,
        grad_wmix,
        small_summed[1],
        small_summed[2],
        grad_wout.T,
        small_summed[3],
        grad_gate,
        grad_up,
        grad_down.T,
        rms_stats,
    )


def solution(mesh):
    rows = P(("dp", "tensor"), None)
    flat = P(("dp", "tensor"))
    first, second = P("dp", "tensor"), P("tensor", "dp")
    return jax.shard_map(
        functools.partial(shards, mesh.shape["dp"], mesh.shape["tensor"]),
        mesh=mesh,
        in_specs=(
            rows, rows, flat, P(), P(), flat, first, first, first, flat, flat, second, flat, first, first, second,
        ),
        out_specs=(
            rows, rows, flat, first, first, first, flat, flat, second, flat, first, first, second, P(),
        ),
        check_vma=False,
    )
```

time: 2140 us -> 953 us (0.45)
  waiting for transfers between devices: 1460 us -> 386 us
  blocking collectives: 219 us -> 12.5 us
  local copies, waits for them, and re-layouts: 219 us -> 41.2 us
  starting transfers between devices: 1.51 us -> 179 us
  Pallas kernels: 0 us -> 73.5 us
  other arithmetic: 91.4 us -> 120 us
    reduce_scatter x11 -> x4, waiting for transfers between devices: 1030 us -> 0.01 us  [tensor_reduce(): lax.psum_scatter(partial_term.astype(jnp.bfloat16), 'tensor', scatter_dim...]
    ppermute x0 -> x84, waiting for transfers between devices: none -> 386 us  [send(): arrived = lax.ppermute(values, 'dp', pairs)]
    all_gather x7 -> x0, waiting for transfers between devices: 366 us -> none  [the longest x1 95.2 us: shards(): lax.all_gather(w_down, 'dp', axis=1, tiled=True)]
    ppermute x0 -> x84, starting transfers between devices: none -> 178 us  [send(): arrived = lax.ppermute(values, 'dp', pairs)]
    slice x153 -> x4, local copies, waits for them, and re-layouts: 136 us -> 2.69 us  [the longest x1 1.25 us: shards(): rms_stats = jnp.sqrt(totals[:3] / (jnp.maximum(totals[3], 1.0) * D))]
    all_gather x4 -> x0, blocking collectives: 122 us -> none  [the longest x1 30.8 us: shards(): lax.all_gather(head_decay * tail_decay[:, 0], 'dp', axis=0, tiled=True)]
    unnamed x2 -> x0, blocking collectives: 85.1 us -> none
    pallas_call x0 -> x7, Pallas kernels: none -> 73.5 us  [the longest x2 39 us: flat_exchange(): pl.pallas_call(functools.partial(flat_exchange_kernel, dp, tp, reduce), o...]
  transfers between devices with their start and end apart: 22 -> 92, of which waited for: 20 -> 34; matrix products, arithmetic and copies ran while one was open for 11% -> 24% of each run, Pallas kernels for 0% -> 6%
where the time goes in v1:
time: 953 us; the launch traced here: 941 us
  waiting for transfers between devices  386 us (41%)
  starting transfers between devices  179 us (19%)
  other arithmetic  120 us (13%)
  matrix products  111 us (12%)
  Pallas kernels  73.5 us (8%)
  local copies, waits for them, and re-layouts  41.2 us (4%)
  between operations  17.8 us (2%)
  blocking collectives  12.5 us (1%)
    ppermute x84, waiting for transfers between devices, send(): arrived = lax.ppermute(values, 'dp', pairs)  386 us
    ppermute x84, starting transfers between devices, send(): arrived = lax.ppermute(values, 'dp', pairs)  178 us
    dot_general x14, matrix products, dot(): return jnp.dot(operand, matrix, preferred_element_type=jnp.float32)  46.2 us
    pallas_call x2, Pallas kernels, flat_exchange(): pl.pallas_call(functools.partial(flat_exchange_kernel, dp, tp, reduce), o...  39 us
    convert_element_type x23, other arithmetic, collect(): (slots[r] + arrived.astype(jnp.float32)).astype(jnp.bfloat16)  37.1 us
    dot_general x14, matrix products, inner_rows(): lax.dot_general(operand, matrix, (((0,), (0,)), ((), ())), preferred_elem...  32.6 us
    dot_general x14, matrix products, times_transposed(): lax.dot_general(operand, matrix, (((1,), (1,)), ((), ())), preferred_elem...  32.2 us
    unnamed x316, local copies, waits for them, and re-layouts  23.8 us
  transfers between devices with their start and end apart: 92, of which 34 were waited for; matrix products, arithmetic and copies ran while one was open for 24% of the time, Pallas kernels for 6%

profile of v1, /device:TPU:0, one launch (start us, length us, event | category | flops | bytes accessed | tf_op | source)
XLA Modules:
  0.0 941.1 jit_solution(5509803751869767463)
XLA Ops:
  17.9 23.8 %flat_gather.1 = f32[32,8,128]{2,1,0:T(8,128)} custom-call(f32[1,8,128]{2,1,0:T(8,128)} %fusion.93.x_ref), custom_call_target="tpu_custom_call" | custom-call | bytes 16777216 | tf_op jit(solution)/shard_map/flat_gather/pallas_call | solution.py:108
  56.3 18.7 %collective-permute-done.2 = bf16[256,1536]{1,0:T(8,128)(2,1)} collective-permute-done((bf16[256,1536]{1,0:T(8,128)(2,1)S(1)}, bf16[256,1536]{1,0:T(8,128)(2,1)}, u32[]{:S(2)}, u32[]{:S(2)}) %collective-permute-start.2) | collective-permute-done | bytes 786464 | tf_op jit(solution)/shard_map/ppermute | solution.py:372
  84.6 16.7 %collective-permute-done.8 = bf16[256,512]{0,1:T(8,128)(2,1)S(1)} collective-permute-done((bf16[256,512]{0,1:T(8,128)(2,1)}, bf16[256,512]{0,1:T(8,128)(2,1)S(1)}, u32[]{:S(2)}, u32[]{:S(2)}) %collective-permute-start.8) | collective-permute-done | bytes 262176 | tf_op jit(solution)/shard_map/ppermute | solution.py:372
  141.1 9.7 %collective-permute-done.16 = bf16[256,1408]{1,0:T(8,128)(2,1)} collective-permute-done((bf16[256,1408]{1,0:T(8,128)(2,1)S(1)}, bf16[256,1408]{1,0:T(8,128)(2,1)}, u32[]{:S(2)}, u32[]{:S(2)}) %collective-permute-start.16) | collective-permute-done | bytes 720928 | tf_op jit(solution)/shard_map/ppermute | solution.py:372
  156.2 10.7 %collective-permute-done.17 = bf16[256,1408]{1,0:T(8,128)(2,1)S(1)} collective-permute-done((bf16[256,1408]{1,0:T(8,128)(2,1)}, bf16[256,1408]{1,0:T(8,128)(2,1)S(1)}, u32[]{:S(2)}, u32[]{:S(2)}) %collective-permute-start.17) | collective-permute-done | bytes 720928 | tf_op jit(solution)/shard_map/ppermute | solution.py:372
  168.1 17.0 %collective-permute-done.6 = bf16[1024,1536]{1,0:T(8,128)(2,1)} collective-permute-done((bf16[1024,1536]{1,0:T(8,128)(2,1)}, bf16[1024,1536]{1,0:T(8,128)(2,1)}, u32[]{:S(2)}, u32[]{:S(2)}) %collective-permute-start.6) | collective-permute-done | bytes 3145760 | tf_op jit(solution)/shard_map/ppermute | solution.py:372
  200.3 9.4 carry_fwd.1.carry_ref
  238.5 13.6 %collective-permute-done.22 = bf16[256,1408]{1,0:T(8,128)(2,1)S(1)} collective-permute-done((bf16[256,1408]{1,0:T(8,128)(2,1)S(1)}, bf16[256,1408]{1,0:T(8,128)(2,1)S(1)}, u32[]{:S(2)}, u32[]{:S(2)}) %collective-permute-start.22) | collective-permute-done | bytes 720928 | tf_op jit(solution)/shard_map/ppermute | solution.py:372
  255.0 41.0 %collective-permute-done.20 = bf16[1024,1408]{1,0:T(8,128)(2,1)S(1)} collective-permute-done((bf16[1024,1408]{1,0:T(8,128)(2,1)S(1)}, bf16[1024,1408]{1,0:T(8,128)(2,1)S(1)}, u32[]{:S(2)}, u32[]{:S(2)}) %collective-permute-start.20) | collective-permute-done | bytes 2883616 | tf_op jit(solution)/shard_map/ppermute | solution.py:372
  301.7 11.0 %collective-permute-done.28 = bf16[256,1408]{0,1:T(8,128)(2,1)S(1)} collective-permute-done((bf16[256,1408]{0,1:T(8,128)(2,1)S(1)}, bf16[256,1408]{0,1:T(8,128)(2,1)S(1)}, u32[]{:S(2)}, u32[]{:S(2)}) %collective-permute-start.28) | collective-permute-done | bytes 720928 | tf_op jit(solution)/shard_map/ppermute | solution.py:372
  333.5 14.2 %collective-permute-done.30 = bf16[2,256,1408]{1,2,0:T(8,128)(2,1)} collective-permute-done((bf16[2,256,1408]{1,2,0:T(8,128)(2,1)}, bf16[2,256,1408]{1,2,0:T(8,128)(2,1)}, u32[]{:S(2)}, u32[]{:S(2)}) %collective-permute-start.30) | collective-permute-done | bytes 1441824 | tf_op jit(solution)/shard_map/ppermute | solution.py:372
  352.0 28.5 %collective-permute-done.31 = bf16[2,256,1408]{1,2,0:T(8,128)(2,1)} collective-permute-done((bf16[2,256,1408]{1,2,0:T(8,128)(2,1)}, bf16[2,256,1408]{1,2,0:T(8,128)(2,1)}, u32[]{:S(2)}, u32[]{:S(2)}) %collective-permute-start.31) | collective-permute-done | bytes 1441824 | tf_op jit(solution)/shard_map/ppermute | solution.py:372
  386.3 8.2 collective-permute-done.27
  475.6 34.2 %collective-permute-done.38 = bf16[1024,1408]{1,0:T(8,128)(2,1)S(1)} collective-permute-done((bf16[1024,1408]{1,0:T(8,128)(2,1)}, bf16[1024,1408]{1,0:T(8,128)(2,1)S(1)}, u32[]{:S(2)}, u32[]{:S(2)}) %collective-permute-start.38) | collective-permute-done | bytes 2883616 | tf_op jit(solution)/shard_map/ppermute | solution.py:372
  516.9 54.7 %collective-permute-done.35 = bf16[1024,1408]{1,0:T(8,128)(2,1)} collective-permute-done((bf16[1024,1408]{1,0:T(8,128)(2,1)}, bf16[1024,1408]{1,0:T(8,128)(2,1)}, u32[]{:S(2)}, u32[]{:S(2)}) %collective-permute-start.35) | collective-permute-done | bytes 2883616 | tf_op jit(solution)/shard_map/ppermute | solution.py:372
  584.8 9.8 %collective-permute-done.42 = bf16[256,1408]{1,0:T(8,128)(2,1)} collective-permute-done((bf16[256,1408]{1,0:T(8,128)(2,1)}, bf16[256,1408]{1,0:T(8,128)(2,1)}, u32[]{:S(2)}, u32[]{:S(2)}) %collective-permute-start.42) | collective-permute-done | bytes 720928 | tf_op jit(solution)/shard_map/ppermute | solution.py:372
  614.4 12.0 %collective-permute-done.44 = bf16[256,1408]{1,0:T(8,128)(2,1)S(1)} collective-permute-done((bf16[256,1408]{1,0:T(8,128)(2,1)S(1)}, bf16[256,1408]{1,0:T(8,128)(2,1)S(1)}, u32[]{:S(2)}, u32[]{:S(2)}) %collective-permute-start.44) | collective-permute-done | bytes 720928 | tf_op jit(solution)/shard_map/ppermute | solution.py:372
  649.5 8.8 collective-permute-start.46
  674.6 8.2 collective-permute-done.47
  695.4 8.9 collective-permute-done.48
  734.7 9.5 %carry_back.1.back_ref = f32[4,512]{1,0:T(4,128)} custom-call(f32[8,512]{1,0:T(8,128)} %get-tuple-element.135.ends_ref, s32[32]{0:T(128)} %multiply_add_fusion.rows_ref, s32[4]{0:T(128)} %get-tuple-element.249.ids_ref), custom_call_target="tpu_custom_call" | custom-call | bytes 16777216 | tf_op jit(solution)/shard_map/carry_back/pallas_call | solution.py:174
  772.7 9.2 collective-permute-done.36
  899.2 8.0 collective-permute-done.83
  912.3 15.2 %flat_reduce.1 = f32[1,8,128]{2,1,0:T(8,128)} custom-call(f32[32,8,128]{2,1,0:T(8,128)} %bitcast.115), custom_call_target="tpu_custom_call" | custom-call | bytes 16777216 | tf_op jit(solution)/shard_map/flat_reduce/pallas_call | solution.py:108
  (668 shorter events, 522.5 us)
Async XLA Ops:
  7.2 160.9 %all-gather.5.cloned.1.call-start = ((), (), s32[]{:S(2)}) async-start(), calls=%async_computation.4 | async-start | bytes 2621440 | tf_op jit(solution)/shard_map/all_gather | solution.py:57
  10.1 40.7 %collective-permute-start = (bf16[256,1536]{1,0:T(8,128)(2,1)S(1)}, bf16[256,1536]{1,0:T(8,128)(2,1)S(1)}, u32[]{:S(2)}, u32[]{:S(2)}) collective-permute-start(bf16[256,1536]{1,0:T(8,128)(2,1)S(1)} %constant_dynamic-update-slice_fusion.16), channel_id=1, source_target_pairs={{0,8},{4,12},{8,16},{12,20},{16,24},{20,28},{1,9},{5,13},{9,17},{1... | collective-permute-start | bytes 2359304 | tf_op jit(solution)/shard_map/ppermute | solution.py:372
  15.2 37.2 %collective-permute-start.1 = (bf16[256,1536]{1,0:T(8,128)(2,1)S(1)}, bf16[256,1536]{1,0:T(8,128)(2,1)S(1)}, u32[]{:S(2)}, u32[]{:S(2)}) collective-permute-start(bf16[256,1536]{1,0:T(8,128)(2,1)S(1)} %constant_dynamic-update-slice_fusion.16), channel_id=1, source_target_pairs={{8,0},{12,4},{16,8},{20,12},{24,16},{28,20},{9,1},{13,5},{17,9},{2... | collective-permute-start | bytes 2359304 | tf_op jit(solution)/shard_map/ppermute | solution.py:372
  54.7 266.4 %reduce-scatter.5.cloned.1.call-start = ((), (), s32[]{:S(2)}) async-start(), calls=%async_computation.5 | async-start | bytes 2621440 | tf_op jit(solution)/shard_map/reduce_scatter | solution.py:61
  55.6 47.1 %collective-permute-start.5 = (bf16[256,1536]{1,0:T(8,128)(2,1)}, bf16[256,1536]{1,0:T(8,128)(2,1)S(1)}, u32[]{:S(2)}, u32[]{:S(2)}) collective-permute-start(bf16[256,1536]{1,0:T(8,128)(2,1)} %collective-permute-done.4), channel_id=1, source_target_pairs={{16,24},{20,28},{17,25},{21,29},{18,26},{22,30},{19,27},{23,31}} | collective-permute-start | bytes 2359304 | tf_op jit(solution)/shard_map/ppermute | solution.py:372
  113.8 71.3 %collective-permute-start.6 = (bf16[1024,1536]{1,0:T(8,128)(2,1)}, bf16[1024,1536]{1,0:T(8,128)(2,1)}, u32[]{:S(2)}, u32[]{:S(2)}) collective-permute-start(bf16[1024,1536]{1,0:T(8,128)(2,1)} %pad_maximum_fusion), channel_id=1, source_target_pairs={{0,4},{4,0},{8,12},{12,8},{16,20},{20,16},{24,28},{28,24},{1,5},{5... | collective-permute-start | bytes 9437192 | tf_op jit(solution)/shard_map/ppermute | solution.py:372
  153.3 72.5 %collective-permute-start.13 = (bf16[1024,512]{0,1:T(8,128)(2,1)}, bf16[1024,512]{0,1:T(8,128)(2,1)}, u32[]{:S(2)}, u32[]{:S(2)}) collective-permute-start(bf16[1024,512]{0,1:T(8,128)(2,1)} %pad_maximum_fusion.10), channel_id=1, source_target_pairs={{0,4},{4,0},{8,12},{12,8},{16,20},{20,16},{24,28},{28,24},{1,5},{5... | collective-permute-start | bytes 3145736 | tf_op jit(solution)/shard_map/ppermute | solution.py:372
  229.4 165.1 %all-gather.7.cloned.1.call-start = ((), (), s32[]{:S(2)}) async-start(), calls=%async_computation.6 | async-start | bytes 2621440 | tf_op jit(solution)/shard_map/all_gather | solution.py:57
  231.9 64.0 %collective-permute-start.20 = (bf16[1024,1408]{1,0:T(8,128)(2,1)S(1)}, bf16[1024,1408]{1,0:T(8,128)(2,1)S(1)}, u32[]{:S(2)}, u32[]{:S(2)}) collective-permute-start(bf16[1024,1408]{1,0:T(8,128)(2,1)S(1)} %pad_maximum_fusion.1), channel_id=1, source_target_pairs={{0,4},{4,0},{8,12},{12,8},{16,20},{20,16},{24,28},{28,24},{1,5},{5... | collective-permute-start | bytes 8650760 | tf_op jit(solution)/shard_map/ppermute | solution.py:372
  252.1 44.8 %collective-permute-start.23 = (bf16[256,1408]{1,0:T(8,128)(2,1)S(1)}, bf16[256,1408]{1,0:T(8,128)(2,1)}, u32[]{:S(2)}, u32[]{:S(2)}) collective-permute-start(bf16[256,1408]{1,0:T(8,128)(2,1)S(1)} %collective-permute-done.22), channel_id=1, source_target_pairs={{8,0},{12,4},{16,8},{20,12},{9,1},{13,5},{17,9},{21,13},{10,2},{14... | collective-permute-start | bytes 2162696 | tf_op jit(solution)/shard_map/ppermute | solution.py:372
  253.4 44.8 %collective-permute-start.25 = (bf16[256,1408]{1,0:T(8,128)(2,1)S(1)}, bf16[256,1408]{1,0:T(8,128)(2,1)}, u32[]{:S(2)}, u32[]{:S(2)}) collective-permute-start(bf16[256,1408]{1,0:T(8,128)(2,1)S(1)} %collective-permute-done.21), channel_id=1, source_target_pairs={{8,16},{12,20},{16,24},{20,28},{9,17},{13,21},{17,25},{21,29},{10,... | collective-permute-start | bytes 2162696 | tf_op jit(solution)/shard_map/ppermute | solution.py:372
  324.4 93.4 %all-gather.9.cloned.1.call-start = ((), (), s32[]{:S(2)}) async-start(), calls=%async_computation.8 | async-start | bytes 2621440 | tf_op jit(solution)/shard_map/all_gather | solution.py:57
  332.4 62.1 %collective-permute-start.27 = (bf16[1024,1408]{1,0:T(8,128)(2,1)}, bf16[1024,1408]{1,0:T(8,128)(2,1)}, u32[]{:S(2)}, u32[]{:S(2)}) collective-permute-start(bf16[1024,1408]{1,0:T(8,128)(2,1)} %pad_maximum_fusion.2), channel_id=1, source_target_pairs={{0,4},{4,0},{8,12},{12,8},{16,20},{20,16},{24,28},{28,24},{1,5},{5... | collective-permute-start | bytes 8650760 | tf_op jit(solution)/shard_map/ppermute | solution.py:372
  351.9 228.5 %reduce-scatter.7.cloned.1.call-start = ((), (), s32[]{:S(2)}) async-start(), calls=%async_computation.7 | async-start | bytes 2621440 | tf_op jit(solution)/shard_map/reduce_scatter | solution.py:61
  437.7 142.8 %reduce-scatter.9.cloned.1.call-start = ((), (), s32[]{:S(2)}) async-start(), calls=%async_computation.9 | async-start | bytes 2621440 | tf_op jit(solution)/shard_map/reduce_scatter | solution.py:61
  444.1 65.6 %collective-permute-start.38 = (bf16[1024,1408]{1,0:T(8,128)(2,1)}, bf16[1024,1408]{1,0:T(8,128)(2,1)S(1)}, u32[]{:S(2)}, u32[]{:S(2)}) collective-permute-start(bf16[1024,1408]{1,0:T(8,128)(2,1)} %convolution_convert_fusion.3), channel_id=1, source_target_pairs={{0,4},{4,0},{8,12},{12,8},{16,20},{20,16},{24,28},{28,24},{1,5},{5... | collective-permute-start | bytes 8650760 | tf_op jit(solution)/shard_map/ppermute | solution.py:372
  460.3 254.2 %all-gather.11.cloned.1.call-start = ((), (), s32[]{:S(2)}) async-start(), calls=%async_computation.10 | async-start | bytes 2621440 | tf_op jit(solution)/shard_map/all_gather | solution.py:57
  465.8 105.9 %collective-permute-start.35 = (bf16[1024,1408]{1,0:T(8,128)(2,1)}, bf16[1024,1408]{1,0:T(8,128)(2,1)}, u32[]{:S(2)}, u32[]{:S(2)}) collective-permute-start(bf16[1024,1408]{1,0:T(8,128)(2,1)} %convolution_convert_fusion.5), channel_id=1, source_target_pairs={{0,4},{4,0},{8,12},{12,8},{16,20},{20,16},{24,28},{28,24},{1,5},{5... | collective-permute-start | bytes 8650760 | tf_op jit(solution)/shard_map/ppermute | solution.py:372
  509.9 63.9 %collective-permute-start.41 = (bf16[256,1408]{1,0:T(8,128)(2,1)S(1)}, bf16[256,1408]{1,0:T(8,128)(2,1)S(1)}, u32[]{:S(2)}, u32[]{:S(2)}) collective-permute-start(bf16[256,1408]{1,0:T(8,128)(2,1)S(1)} %fusion.6), channel_id=1, source_target_pairs={{0,8},{4,12},{1,9},{5,13},{2,10},{6,14},{3,11},{7,15}} | collective-permute-start | bytes 2162696 | tf_op jit(solution)/shard_map/ppermute | solution.py:372
  514.9 132.2 %collective-permute-start.39 = (bf16[1024,1408]{1,0:T(8,128)(2,1)}, bf16[1024,1408]{1,0:T(8,128)(2,1)}, u32[]{:S(2)}, u32[]{:S(2)}) collective-permute-start(bf16[1024,1408]{1,0:T(8,128)(2,1)} %convolution_convert_fusion.4), channel_id=1, source_target_pairs={{0,4},{4,0},{8,12},{12,8},{16,20},{20,16},{24,28},{28,24},{1,5},{5... | collective-permute-start | bytes 8650760 | tf_op jit(solution)/shard_map/ppermute | solution.py:372
  583.9 325.1 %reduce-scatter.11.cloned.1.call-start = ((), (), s32[]{:S(2)}) async-start(), calls=%async_computation.11 | async-start | bytes 2621440 | tf_op jit(solution)/shard_map/reduce_scatter | solution.py:61
  707.8 78.5 %collective-permute-start.66 = (bf16[256,1408]{1,0:T(8,128)(2,1)}, bf16[256,1408]{1,0:T(8,128)(2,1)}, u32[]{:S(2)}, u32[]{:S(2)}) collective-permute-start(bf16[256,1408]{1,0:T(8,128)(2,1)} %get-tuple-element.170), channel_id=1, source_target_pairs={{16,8},{20,12},{24,16},{28,20},{17,9},{21,13},{25,17},{29,21},{18,... | collective-permute-start | bytes 2162696 | tf_op jit(solution)/shard_map/ppermute | solution.py:372
  709.5 82.5 %collective-permute-start.50 = (bf16[256,1408]{1,0:T(8,128)(2,1)}, bf16[256,1408]{1,0:T(8,128)(2,1)}, u32[]{:S(2)}, u32[]{:S(2)}) collective-permute-start(bf16[256,1408]{1,0:T(8,128)(2,1)} %get-tuple-element.154), channel_id=1, source_target_pairs={{0,8},{4,12},{8,16},{12,20},{16,24},{20,28},{1,9},{5,13},{9,17},{1... | collective-permute-start | bytes 2162696 | tf_op jit(solution)/shard_map/ppermute | solution.py:372
  769.9 34.4 %collective-permute-start.40 = (bf16[1024,512]{1,0:T(8,128)(2,1)S(1)}, bf16[1024,512]{1,0:T(8,128)(2,1)S(1)}, u32[]{:S(2)}, u32[]{:S(2)}) collective-permute-start(bf16[1024,512]{1,0:T(8,128)(2,1)S(1)} %convolution_convert_fusion.11), channel_id=1, source_target_pairs={{0,4},{4,0},{8,12},{12,8},{16,20},{20,16},{24,28},{28,24},{1,5},{5... | collective-permute-start | bytes 3145736 | tf_op jit(solution)/shard_map/ppermute | solution.py:372
  (196 other events, 3343.9 us)
Sparse Core Ops, SparseCore 0:
  54.8 24.5 all-gather.4
  229.5 29.2 reduce-scatter.4
  324.5 20.2 all-gather.6
  352.1 25.1 all-gather.8
  437.8 30.3 reduce-scatter.6
  470.6 31.1 reduce-scatter.8
  584.0 21.7 all-gather.10
  766.8 29.7 reduce-scatter.10
